TPU v7x, 256 devices: a whole 4x4x8 slice. The times are simulated.
256 devices in a mesh: seq: 128 (over y, x, z), head: 2 (over core).
Axes of the slice: x: 4, y: 4, z: 8, core: 2. Of those that a mesh axis runs over, the one named last changes fastest.
Arguments:
- tokens: bfloat16 [32768, 2048], P('seq'), may hold values from -6 to 6
- dest: int32 [32768], P('seq'), may hold values from 0 to 32767, as said below
- segment_ids: int32 [32768], P('seq'), may hold values from 0 to 255, never falling along the last dimension, each value on 1 to 1024 neighbouring positions
- gain: float32 [2048], replicated, may hold values from 0.1 to 1.9
- w_qkv: bfloat16 [2048, 3, 1024], P(None, None, 'head')
- w_out: bfloat16 [1024, 2048], P('head'), may hold values from -0.1875 to 0.1875
Outputs:
- layer_out: bfloat16 [32768, 2048], P('seq', 'head')
Inputs may be any that keep to these rules, and one draw needn't show every extreme that they name: dest is a permutation of the sequence positions; the rows of one shard send exactly 2 rows to each shard's block of 256 positions.
All inputs are finite; a program needn't handle non-finite values.
Results may differ from a plain program's by a relative error of at most 0.017.
The roundings to bfloat16 on the way count: a program that leaves them out, or rounds other values in their place, can miss the bound.
Values may be sent and summed in bfloat16 or wider, within the bound.
A program may use at most 128 MiB of HBM per device.

v0:
```python
import functools
import math

import jax
import jax.numpy as jnp
from jax import lax
from jax.experimental import pallas as pl
from jax.experimental.pallas import tpu as pltpu
from jax.sharding import PartitionSpec as P

MESH = pl.DeviceIdType.MESH
F32 = jnp.float32
BF16 = jnp.bfloat16
NX, NY, NZ = 4, 4, 8
NXY = NX * NY
SHARDS = NXY * NZ
ROWS = 256
WIDTH = 2048
DH = 128
GROUP = 512
HEADS = 4
CHUNKS = WIDTH // 128
SCORE = DH ** (-0.5) * math.log2(math.e)
WAVES = ((0,), (1, 7), (2, 6), (4,), (3, 5))
ORDER = tuple(oz for wave in WAVES for oz in wave)
EARLY = 4


def iota(shape, dim):
    return lax.broadcasted_iota(jnp.int32, shape, dim)


def mm(a, b):
    return jnp.dot(a, b, preferred_element_type=F32)


def mm_nt(a, b):
    return lax.dot_general(a, b, (((1,), (1,)), ((), ())), preferred_element_type=F32)


def layer(
    tok_hbm, dest_ref, seg_ref, gain_ref, wqkv_hbm, wout_hbm, out_ref,
    tok, wqkv, wo_own, wo_sib, stage, send, recv, recv_sib, xs,
    posa_src, posa, posb_src, posb, place, pool,
    k_own, v_own, q_raw, q_own, ids_src, ids_halo, k_halo, v_halo,
    crs_src, crs, line_up, far, bias, top, tot, acc, prob, at_own, at_sib,
    load_sem, row_send, row_recv, sib_send, sib_recv, go,
    pos_sem, ids_sem, k_send, k_recv, v_send, v_recv, crs_sem, wo_sem, at_sem,
):
    me = lax.axis_index("seq")
    core = lax.axis_index("head")
    other = 1 - core
    xy, z = me // NZ, me % NZ
    y, x = xy // NX, xy % NX
    left, right = (me + SHARDS - 1) % SHARDS, (me + 1) % SHARDS

    def remote(src, dst, send_sem, recv_sem, seq, head):
        return pltpu.make_async_remote_copy(
            src_ref=src, dst_ref=dst, send_sem=send_sem, recv_sem=recv_sem,
            device_id=(seq, head), device_id_type=MESH,
        )

    def drain(ref, sem):
        pltpu.make_async_copy(ref, ref, sem).wait()

    load_tok = pltpu.make_async_copy(tok_hbm, tok, load_sem.at[0])
    load_tok.start()
    load_w = [
        pltpu.make_async_copy(wqkv_hbm.at[part], wqkv.at[part], load_sem.at[1 + part])
        for part in range(3)
    ]
    for part in (1, 2, 0):
        load_w[part].start()
    load_wo = pltpu.make_async_copy(
        wout_hbm.at[:, pl.ds(pl.multiple_of(core * 1024, 1024), 1024)], wo_own, load_sem.at[4]
    )
    load_wo.start()

    barrier = pltpu.get_barrier_semaphore()
    for o in range(1, NZ):
        pl.semaphore_signal(
            barrier, inc=1, device_id=(xy * NZ + (z + o) % NZ, core), device_id_type=MESH
        )

    def greet(o, carry):
        pl.semaphore_signal(
            barrier, inc=1, device_id=(((xy + o) % NXY) * NZ + z, core), device_id_type=MESH
        )
        return carry

    lax.fori_loop(1, NXY, greet, 0)
    pl.semaphore_signal(barrier, inc=1, device_id=(me, other), device_id_type=MESH)

    dest = dest_ref[...]
    shard = jnp.right_shift(dest, 8).astype(F32)
    slot = jnp.bitwise_and(dest, 255).astype(F32)
    by_lane = jnp.broadcast_to(shard, (ROWS, ROWS))
    by_row = by_lane.T
    earlier = (by_lane == by_row) & (iota((ROWS, ROWS), 0) < iota((ROWS, ROWS), 1))
    rank = jnp.sum(jnp.where(earlier, 1.0, 0.0), axis=0, keepdims=True)
    hit = iota((SHARDS, ROWS), 0).astype(F32) == shard
    mine = hit & (rank == core.astype(F32))
    pick = jnp.where(mine, 1.0, 0.0).astype(BF16)
    pair = iota((8, ROWS), 0).astype(F32) == rank
    slots = jnp.where(pair, slot, 0.0).astype(BF16)
    posa_src[...] = mm_nt(slots, jnp.where(hit, 1.0, 0.0).astype(BF16))[0:2, :]
    load_tok.wait()
    gain = gain_ref[...]
    rows = mm(pick, tok[...])
    scale = lax.rsqrt(jnp.sum(rows * rows, axis=-1, keepdims=True) * (1.0 / WIDTH) + 1e-05)
    for j in range(CHUNKS):
        cols = slice(j * 128, (j + 1) * 128)
        stage[pl.ds(j, SHARDS, stride=CHUNKS), :] = rows[:, cols] * scale * gain[:, cols]
    send[...] = stage[...].reshape(SHARDS, CHUNKS, 128).astype(BF16)

    pl.semaphore_wait(barrier, NZ - 1 + NXY)
    for o in range(1, NZ):
        pl.semaphore_signal(
            go.at[NZ - o], inc=1, device_id=(xy * NZ + (z + o) % NZ, core), device_id_type=MESH
        )

    posa[z] = posa_src[...]
    for o in range(1, NZ):
        remote(
            posa_src, posa.at[z], pos_sem.at[0], pos_sem.at[1], xy * NZ + (z + o) % NZ, core,
        ).start()

    def send_rows(first, wave):
        def body(i, carry):
            at = ((y + i // NX) % NY) * NX + (x + i % NX) % NX
            for oz in wave:
                group = ORDER.index(oz)
                peer = at * NZ + (z + oz) % NZ
                remote(
                    send.at[peer], recv.at[group * NXY + xy], row_send, row_recv.at[group],
                    peer, core,
                ).start()
            return carry

        lax.fori_loop(first, NXY, body, 0)

    pltpu.make_async_copy(send.at[me], recv.at[xy], row_recv.at[0]).start()
    send_rows(1, WAVES[0])
    for number, wave in enumerate(WAVES[1:]):
        for oz in wave:
            pl.semaphore_wait(go.at[oz], 1)
        send_rows(0, wave)
        if number == 1:
            drain(posa.at[pl.ds(0, NZ - 1)], pos_sem.at[1])
            for oz in range(NZ):
                for k in range(2):
                    posb_src[k * NZ + oz:k * NZ + oz + 1, :] = posa[oz, k:k + 1, :]
            posb[pl.ds(pl.multiple_of(xy * 16, 16), 16), :] = posb_src[...]

            def send_pos(o, carry):
                remote(
                    posb_src, posb.at[pl.ds(pl.multiple_of(xy * 16, 16), 16)], pos_sem.at[2],
                    pos_sem.at[3], ((xy + o) % NXY) * NZ + z, core,
                ).start()
                return carry

            lax.fori_loop(1, NXY, send_pos, 0)

    def unpack(group, landed, line):
        part = pl.ds(group * NXY * CHUNKS, NXY * CHUNKS)
        stage[part, :] = (
            landed[group * NXY:(group + 1) * NXY].astype(F32).reshape(NXY * CHUNKS, 128)
        )
        for j in range(CHUNKS):
            xs[line:line + NXY, j * 128:(j + 1) * 128] = (
                stage[pl.ds(group * NXY * CHUNKS + j, NXY, stride=CHUNKS), :].astype(BF16)
            )

    def collect(first):
        base = (first // EARLY) * 128
        for group in range(first, first + EARLY):
            block = pl.ds(group * NXY, NXY)
            drain(recv.at[block], row_recv.at[group])
            remote(
                recv.at[block], recv_sib.at[block], sib_send, sib_recv.at[group], me, other
            ).start()
            unpack(group, recv, base + (group - first) * NXY)
        for group in range(first, first + EARLY):
            drain(recv_sib.at[pl.ds(group * NXY, NXY)], sib_recv.at[group])
            unpack(group, recv_sib, base + 64 + (group - first) * NXY)

    def project(part, own, half):
        lines = slice(half * 128, (half + 1) * 128)
        own[lines, :] = mm(xs[lines, :], wqkv[part]).astype(BF16)

    def send_halo(own, halo, half, send_sem, recv_sem):
        lines = pl.ds(half * 128, 128)
        for side, peer in ((1, left), (0, right)):
            remote(
                own.at[lines], halo.at[side, lines], send_sem, recv_sem.at[side, half], peer, core
            ).start()

    collect(0)
    load_w[1].wait()
    load_w[2].wait()
    project(1, k_own, 0)
    send_halo(k_own, k_halo, 0, k_send, k_recv)
    project(2, v_own, 0)
    send_halo(v_own, v_halo, 0, v_send, v_recv)

    drain(posb.at[pl.ds(0, 240)], pos_sem.at[3])
    pieces = []
    for first in (0, EARLY):
        for who in (core, other):
            for oz in ORDER[first:first + EARLY]:
                pieces.append(posb[pl.ds(who * NZ + (z + NZ - oz) % NZ, NXY, stride=16), :])
    table = jnp.concatenate(pieces, axis=0).astype(BF16)
    my_lane = jnp.where(iota((8, 128), 1) == me, 1.0, 0.0).astype(BF16)
    pos_row = mm_nt(my_lane, table)[0:1, :]
    where_to = jnp.where(iota((ROWS, ROWS), 0).astype(F32) == pos_row, 1.0, 0.0).astype(BF16)
    place[...] = where_to
    seg = seg_ref[...].astype(F32)
    ids_src[...] = mm(jnp.broadcast_to(seg, (8, ROWS)).astype(BF16), where_to)
    for side, peer in ((1, left), (0, right)):
        remote(ids_src, ids_halo.at[side], ids_sem.at[0], ids_sem.at[1], peer, core).start()

    place_int = pos_row.astype(jnp.int32)
    line = iota((128, ROWS), 0)
    spread = jnp.broadcast_to(place_int, (128, ROWS))
    weights = jnp.zeros((128, ROWS), F32)
    start = 0
    for level in range(4):
        count = 16 >> level
        inside = (line >= start) & (line < start + HEADS * count)
        same = jnp.right_shift(spread, 4 + level) == (line - start) % count
        weights = jnp.where(inside & same, 1.0 / (16 << level), weights)
        start += HEADS * count
    pool[...] = weights.astype(BF16)

    line = iota((256, 256), 0)
    head_at, unit = line // 64, line % 16
    level_at = (line % 64) // 16
    origin = jnp.where(
        level_at == 0, head_at * 16 + unit,
        jnp.where(
            level_at == 1, 64 + (unit // 8) * 32 + head_at * 8 + unit % 8,
            jnp.where(
                level_at == 2, 128 + (unit // 4) * 16 + head_at * 4 + unit % 4,
                192 + (unit // 2) * 8 + head_at * 2 + unit % 2,
            ),
        ),
    )
    line_up[...] = jnp.where(iota((256, 256), 1) == origin, 1.0, 0.0).astype(BF16)

    own_col = jnp.broadcast_to(seg, (ROWS, ROWS)).T
    bias[:, 0:ROWS] = jnp.where(own_col == ids_src[0:1, :], 0.0, -jnp.inf)

    collect(EARLY)
    project(1, k_own, 1)
    send_halo(k_own, k_halo, 1, k_send, k_recv)
    project(2, v_own, 1)

    line = iota((128, 128), 0)
    head_of = jnp.where(
        line < 64, line // 16,
        jnp.where(line < 96, (line - 64) // 8, jnp.where(line < 112, (line - 96) // 4, (line - 112) // 2)),
    )
    for which, own in ((0, k_own), (1, v_own)):
        picked = jnp.zeros((128, 128), F32)
        for half in range(2):
            means = mm(pool[...], own[:, half * 256:(half + 1) * 256])
            for sub in range(2):
                picked = jnp.where(
                    head_of == half * 2 + sub, means[:, sub * 128:(sub + 1) * 128], picked
                )
        crs_src[:, which * 128:(which + 1) * 128] = picked.astype(BF16)
    start = 0
    for level in range(4):
        size = 1 << level
        lines = 64 >> level
        group = me // size
        partner = group + 1 - 2 * (group % 2)
        for i in range(size):
            remote(
                crs_src.at[pl.ds(start, lines)],
                crs.at[pl.ds(pl.multiple_of(64 * level + (me % size) * lines, 8), lines)],
                crs_sem.at[0], crs_sem.at[1], partner * size + i, core,
            ).start()
        start += lines
    send_halo(v_own, v_halo, 1, v_send, v_recv)
    remote(
        wout_hbm.at[:, pl.ds(pl.multiple_of(other * 1024, 1024), 1024)], wo_sib,
        wo_sem.at[0], wo_sem.at[1], me, other,
    ).start()

    load_w[0].wait()
    for half in range(2):
        cols = slice(half * 256, (half + 1) * 256)
        q_raw[half] = mm(xs[...], wqkv[0, :, cols]).astype(BF16)
    for half in range(2):
        q_own[half] = mm(place[...], q_raw[half]).astype(BF16)

    def head(ref, h):
        return ref[:, h * 128:(h + 1) * 128]

    def fine(h, keys, mask):
        return mm_nt(q_own[h // 2, :, (h % 2) * 128:(h % 2 + 1) * 128], keys) * SCORE + mask

    for h in range(HEADS):
        score = fine(h, head(k_own, h), bias[:, 0:ROWS])
        best = jnp.max(score, axis=-1, keepdims=True)
        weight = jnp.exp2(score - best)
        tot[h] = jnp.broadcast_to(jnp.sum(weight, axis=-1, keepdims=True), (ROWS, 128))
        top[h] = jnp.broadcast_to(best, (ROWS, 128))
        acc[h] = mm(weight.astype(BF16), head(v_own, h))

    drain(ids_halo, ids_sem.at[1])
    own_col = jnp.broadcast_to(seg, (ROWS, ROWS)).T
    edge = ((me > 0), (me < SHARDS - 1))
    for side in range(2):
        same = own_col == ids_halo[side][0:1, :]
        bias[:, (side + 1) * ROWS:(side + 2) * ROWS] = jnp.where(same & edge[side], 0.0, -jnp.inf)

    for half in range(2):
        for side in range(2):
            drain(k_halo.at[side, pl.ds(half * 128, 128)], k_recv.at[side, half])
    drain(crs, crs_sem.at[1])
    far[...] = mm(line_up[...], crs[...]).astype(BF16)
    lift = (iota((8, 64), 1) // 16 + 4).astype(F32)[0:1, :]

    for h in range(HEADS):
        scores = [
            fine(h, head(k_halo.at[side], h), bias[:, (side + 1) * ROWS:(side + 2) * ROWS])
            for side in range(2)
        ]
        scores.append(fine(h, far[h * 64:(h + 1) * 64, 0:128], lift))
        old = top[h][:, 0:1]
        best = old
        for score in scores:
            best = jnp.maximum(best, jnp.max(score, axis=-1, keepdims=True))
        fade = jnp.exp2(old - best)
        weight = jnp.exp2(scores[2] - best)
        total = tot[h] * fade + jnp.sum(weight, axis=-1, keepdims=True)
        acc[h] = acc[h] * fade + mm(weight.astype(BF16), far[h * 64:(h + 1) * 64, 128:256])
        for side in range(2):
            weight = jnp.exp2(scores[side] - best)
            total = total + jnp.sum(weight, axis=-1, keepdims=True)
            prob[h, side] = weight.astype(BF16)
        tot[h] = total

    load_wo.wait()
    for half in range(2):
        for side in range(2):
            drain(v_halo.at[side, pl.ds(half * 128, 128)], v_recv.at[side, half])
    for half in range(2):
        for h in (half * 2, half * 2 + 1):
            total = acc[h]
            for side in range(2):
                total = total + mm(prob[h, side], head(v_halo.at[side], h))
            at_own[half, :, (h % 2) * 128:(h % 2 + 1) * 128] = (total / tot[h]).astype(BF16)
        remote(
            at_own.at[half], at_sib.at[half], at_sem.at[0], at_sem.at[1 + half], me, other
        ).start()

    drain(wo_sib, wo_sem.at[1])
    for half in range(2):
        drain(at_sib.at[half], at_sem.at[1 + half])
    for part in range(4):
        cols = slice(part * 256, (part + 1) * 256)
        total = jnp.zeros((ROWS, 256), F32)
        for half in range(2):
            lines = slice(half * 256, (half + 1) * 256)
            total = total + mm(at_own[half], wo_own[lines, cols])
            total = total + mm(at_sib[half], wo_sib[lines, cols])
        out_ref[:, cols] = total.astype(BF16)

    drain(send.at[pl.ds(0, SHARDS - 1)], row_send)
    drain(posa.at[pl.ds(0, NZ - 1)], pos_sem.at[0])
    drain(posb.at[pl.ds(0, 240)], pos_sem.at[2])
    drain(ids_halo, ids_sem.at[0])
    drain(recv, sib_send)
    drain(k_halo, k_send)
    drain(v_halo, v_send)
    drain(crs, crs_sem.at[0])
    drain(wo_sib, wo_sem.at[0])
    drain(at_own, at_sem.at[0])


def shards(tokens, dest, segment_ids, gain, w_qkv, w_out):
    vmem = pl.BlockSpec(memory_space=pltpu.VMEM)
    hbm = pl.BlockSpec(memory_space=pl.ANY)
    dma = pltpu.SemaphoreType.DMA
    V = pltpu.VMEM
    return pl.pallas_call(
        layer,
        out_shape=jax.ShapeDtypeStruct((ROWS, 1024), BF16),
        in_specs=[hbm, vmem, vmem, vmem, hbm, hbm],
        out_specs=vmem,
        scratch_shapes=[
            V((ROWS, WIDTH), BF16), V((3, WIDTH, GROUP), BF16), V((GROUP, 1024), BF16),
            V((GROUP, 1024), BF16), V((SHARDS * CHUNKS, 128), F32), V((SHARDS, CHUNKS, 128), BF16),
            V((SHARDS, CHUNKS, 128), BF16), V((SHARDS, CHUNKS, 128), BF16), V((ROWS, WIDTH), BF16),
            V((2, 128), F32), V((NZ, 2, 128), F32), V((16, 128), F32), V((256, 128), F32),
            V((ROWS, ROWS), BF16), V((128, ROWS), BF16),
            V((ROWS, GROUP), BF16), V((ROWS, GROUP), BF16), V((2, ROWS, 256), BF16),
            V((2, ROWS, 256), BF16), V((8, ROWS), F32), V((2, 8, ROWS), F32),
            V((2, ROWS, GROUP), BF16), V((2, ROWS, GROUP), BF16),
            V((128, 256), BF16), V((256, 256), BF16), V((256, 256), BF16), V((256, 256), BF16),
            V((ROWS, 3 * ROWS), F32),
            V((HEADS, ROWS, 128), F32), V((HEADS, ROWS, 128), F32), V((HEADS, ROWS, 128), F32),
            V((HEADS, 2, ROWS, ROWS), BF16), V((2, ROWS, 256), BF16), V((2, ROWS, 256), BF16),
            dma((5,)), dma, dma((NZ,)), dma, dma((NZ,)), pltpu.SemaphoreType.REGULAR((NZ,)),
            dma((4,)), dma((2,)), dma, dma((2, 2)), dma, dma((2, 2)), dma((2,)), dma((2,)), dma((3,)),
        ],
        compiler_params=pltpu.CompilerParams(collective_id=0, has_side_effects=True),
    )(
        tokens, dest.reshape(1, ROWS), segment_ids.reshape(1, ROWS), gain.reshape(1, WIDTH),
        jnp.transpose(w_qkv, (1, 0, 2)), w_out,
    )


def solution(mesh):
    in_specs = (P("seq", None), P("seq"), P("seq"), P(), P(None, None, "head"), P("head", None))
    return jax.shard_map(
        shards, mesh=mesh, in_specs=in_specs, out_specs=P("seq", "head"), check_vma=False
    )
```

profile of v0, /device:TPU:1, one launch (start us, length us, event | category | flops | bytes accessed | tf_op | source)
XLA Modules:
  0.0 50.7 jit_solution(10128739521753701062)
XLA Ops:
  0.0 48.9 %shard_map.64 = bf16[256,1024]{1,0:T(8,128)(2,1)} custom-call(bf16[256,2048]{1,0:T(8,128)(2,1)} %tok_hbm.1, s32[1,256]{1,0:T(1,128)} %bitcast.6, s32[1,256]{1,0:T(1,128)} %bitcast.7, f32[1,2048]{1,0:T(1,128)} %bitcast.5, bf16[3,2048,512]{2,1,0:T(8,128)(2,1)} %bitcast.4, bf16[512,2048]{1,0:T(8,128)(2,1)} %wout_hbm.1), custom_call_target="tpu_custom_call" | custom-call | tf_op jit(solution)/shard_map/pallas_call | solution.py:389
  48.9 1.9 %copy.8 = bf16[256,1024]{1,0:T(8,128)(2,1)} copy(bf16[256,1024]{1,0:T(8,128)(2,1)} %shard_map.64) | data formatting | bytes 1048576
where the time goes:
time: 50.9 us; the launch traced here: 50.7 us
  Pallas kernels  48.9 us (96%)
  local copies, waits for them, and re-layouts  1.87 us (4%)
    pallas_call x1, Pallas kernels, shards(): pl.pallas_call(layer, out_shape=jax.ShapeDtypeStruct((ROWS, 1024), BF16),...  48.9 us
    unnamed x1, local copies, waits for them, and re-layouts  1.87 us

commit v1 on v0

--- a/solution.py
+++ b/solution.py
@@ -21,7 +21,7 @@
 HEADS = 4
 CHUNKS = WIDTH // 128
 SCORE = DH ** (-0.5) * math.log2(math.e)
-WAVES = ((0,), (1, 7), (2, 6), (4,), (3, 5))
+WAVES = ((0,), (1, 7), (2, 6), (3, 5, 4))
 ORDER = tuple(oz for wave in WAVES for oz in wave)
 EARLY = 4
 
@@ -39,8 +39,8 @@
 
 
 def layer(
-    tok_hbm, dest_ref, seg_ref, gain_ref, wqkv_hbm, wout_hbm, out_ref,
-    tok, wqkv, wo_own, wo_sib, stage, send, recv, recv_sib, xs,
+    tok_hbm, dest_hbm, seg_hbm, gain_hbm, wqkv_hbm, wout_hbm, out_ref,
+    dest_ref, seg_ref, gain_ref, tok, wqkv, wo_own, wo_sib, stage, send, recv, recv_sib, xs,
     posa_src, posa, posb_src, posb, place, pool,
     k_own, v_own, q_raw, q_own, ids_src, ids_halo, k_halo, v_halo,
     crs_src, crs, line_up, far, bias, top, tot, acc, prob, at_own, at_sib,
@@ -63,6 +63,14 @@
     def drain(ref, sem):
         pltpu.make_async_copy(ref, ref, sem).wait()
 
+    small = [
+        pltpu.make_async_copy(src, dst, load_sem.at[5 + i])
+        for i, (src, dst) in enumerate(
+            ((dest_hbm, dest_ref), (seg_hbm, seg_ref), (gain_hbm, gain_ref))
+        )
+    ]
+    for load in small:
+        load.start()
     load_tok = pltpu.make_async_copy(tok_hbm, tok, load_sem.at[0])
     load_tok.start()
     load_w = [
@@ -91,6 +99,8 @@
     lax.fori_loop(1, NXY, greet, 0)
     pl.semaphore_signal(barrier, inc=1, device_id=(me, other), device_id_type=MESH)
 
+    for load in small:
+        load.wait()
     dest = dest_ref[...]
     shard = jnp.right_shift(dest, 8).astype(F32)
     slot = jnp.bitwise_and(dest, 255).astype(F32)
@@ -113,6 +123,21 @@
         stage[pl.ds(j, SHARDS, stride=CHUNKS), :] = rows[:, cols] * scale * gain[:, cols]
     send[...] = stage[...].reshape(SHARDS, CHUNKS, 128).astype(BF16)
 
+    line = iota((256, 256), 0)
+    head_at, unit = line // 64, line % 16
+    level_at = (line % 64) // 16
+    origin = jnp.where(
+        level_at == 0, head_at * 16 + unit,
+        jnp.where(
+            level_at == 1, 64 + (unit // 8) * 32 + head_at * 8 + unit % 8,
+            jnp.where(
+                level_at == 2, 128 + (unit // 4) * 16 + head_at * 4 + unit % 4,
+                192 + (unit // 2) * 8 + head_at * 2 + unit % 2,
+            ),
+        ),
+    )
+    line_up[...] = jnp.where(iota((256, 256), 1) == origin, 1.0, 0.0).astype(BF16)
+
     pl.semaphore_wait(barrier, NZ - 1 + NXY)
     for o in range(1, NZ):
         pl.semaphore_signal(
@@ -141,25 +166,24 @@
 
     pltpu.make_async_copy(send.at[me], recv.at[xy], row_recv.at[0]).start()
     send_rows(1, WAVES[0])
-    for number, wave in enumerate(WAVES[1:]):
+    for wave in WAVES[1:]:
         for oz in wave:
             pl.semaphore_wait(go.at[oz], 1)
         send_rows(0, wave)
-        if number == 1:
-            drain(posa.at[pl.ds(0, NZ - 1)], pos_sem.at[1])
-            for oz in range(NZ):
-                for k in range(2):
-                    posb_src[k * NZ + oz:k * NZ + oz + 1, :] = posa[oz, k:k + 1, :]
-            posb[pl.ds(pl.multiple_of(xy * 16, 16), 16), :] = posb_src[...]
-
-            def send_pos(o, carry):
-                remote(
-                    posb_src, posb.at[pl.ds(pl.multiple_of(xy * 16, 16), 16)], pos_sem.at[2],
-                    pos_sem.at[3], ((xy + o) % NXY) * NZ + z, core,
-                ).start()
-                return carry
-
-            lax.fori_loop(1, NXY, send_pos, 0)
+    drain(posa.at[pl.ds(0, NZ - 1)], pos_sem.at[1])
+    for oz in range(NZ):
+        for k in range(2):
+            posb_src[k * NZ + oz:k * NZ + oz + 1, :] = posa[oz, k:k + 1, :]
+    posb[pl.ds(pl.multiple_of(xy * 16, 16), 16), :] = posb_src[...]
+
+    def send_pos(o, carry):
+        remote(
+            posb_src, posb.at[pl.ds(pl.multiple_of(xy * 16, 16), 16)], pos_sem.at[2],
+            pos_sem.at[3], ((xy + o) % NXY) * NZ + z, core,
+        ).start()
+        return carry
+
+    lax.fori_loop(1, NXY, send_pos, 0)
 
     def unpack(group, landed, line):
         part = pl.ds(group * NXY * CHUNKS, NXY * CHUNKS)
@@ -202,6 +226,11 @@
     send_halo(k_own, k_halo, 0, k_send, k_recv)
     project(2, v_own, 0)
     send_halo(v_own, v_halo, 0, v_send, v_recv)
+
+    collect(EARLY)
+    project(1, k_own, 1)
+    send_halo(k_own, k_halo, 1, k_send, k_recv)
+    project(2, v_own, 1)
 
     drain(posb.at[pl.ds(0, 240)], pos_sem.at[3])
     pieces = []
@@ -232,28 +261,8 @@
         start += HEADS * count
     pool[...] = weights.astype(BF16)
 
-    line = iota((256, 256), 0)
-    head_at, unit = line // 64, line % 16
-    level_at = (line % 64) // 16
-    origin = jnp.where(
-        level_at == 0, head_at * 16 + unit,
-        jnp.where(
-            level_at == 1, 64 + (unit // 8) * 32 + head_at * 8 + unit % 8,
-            jnp.where(
-                level_at == 2, 128 + (unit // 4) * 16 + head_at * 4 + unit % 4,
-                192 + (unit // 2) * 8 + head_at * 2 + unit % 2,
-            ),
-        ),
-    )
-    line_up[...] = jnp.where(iota((256, 256), 1) == origin, 1.0, 0.0).astype(BF16)
-
     own_col = jnp.broadcast_to(seg, (ROWS, ROWS)).T
     bias[:, 0:ROWS] = jnp.where(own_col == ids_src[0:1, :], 0.0, -jnp.inf)
-
-    collect(EARLY)
-    project(1, k_own, 1)
-    send_halo(k_own, k_halo, 1, k_send, k_recv)
-    project(2, v_own, 1)
 
     line = iota((128, 128), 0)
     head_of = jnp.where(
@@ -383,15 +392,17 @@
 
 def shards(tokens, dest, segment_ids, gain, w_qkv, w_out):
     vmem = pl.BlockSpec(memory_space=pltpu.VMEM)
-    hbm = pl.BlockSpec(memory_space=pl.ANY)
+    hbm = pl.BlockSpec(memory_space=pltpu.HBM)
     dma = pltpu.SemaphoreType.DMA
+    keep = lambda a: pltpu.with_memory_space_constraint(a, pltpu.HBM)
     V = pltpu.VMEM
     return pl.pallas_call(
         layer,
         out_shape=jax.ShapeDtypeStruct((ROWS, 1024), BF16),
-        in_specs=[hbm, vmem, vmem, vmem, hbm, hbm],
+        in_specs=[hbm] * 6,
         out_specs=vmem,
         scratch_shapes=[
+            V((1, ROWS), jnp.int32), V((1, ROWS), jnp.int32), V((1, WIDTH), F32),
             V((ROWS, WIDTH), BF16), V((3, WIDTH, GROUP), BF16), V((GROUP, 1024), BF16),
             V((GROUP, 1024), BF16), V((SHARDS * CHUNKS, 128), F32), V((SHARDS, CHUNKS, 128), BF16),
             V((SHARDS, CHUNKS, 128), BF16), V((SHARDS, CHUNKS, 128), BF16), V((ROWS, WIDTH), BF16),
@@ -404,13 +415,14 @@
             V((ROWS, 3 * ROWS), F32),
             V((HEADS, ROWS, 128), F32), V((HEADS, ROWS, 128), F32), V((HEADS, ROWS, 128), F32),
             V((HEADS, 2, ROWS, ROWS), BF16), V((2, ROWS, 256), BF16), V((2, ROWS, 256), BF16),
-            dma((5,)), dma, dma((NZ,)), dma, dma((NZ,)), pltpu.SemaphoreType.REGULAR((NZ,)),
+            dma((8,)), dma, dma((NZ,)), dma, dma((NZ,)), pltpu.SemaphoreType.REGULAR((NZ,)),
             dma((4,)), dma((2,)), dma, dma((2, 2)), dma, dma((2, 2)), dma((2,)), dma((2,)), dma((3,)),
         ],
-        compiler_params=pltpu.CompilerParams(collective_id=0, has_side_effects=True),
+        compiler_params=pltpu.CompilerParams(collective_id=0, has_side_effects=True, vmem_limit_bytes=40 * 2**20),
     )(
-        tokens, dest.reshape(1, ROWS), segment_ids.reshape(1, ROWS), gain.reshape(1, WIDTH),
-        jnp.transpose(w_qkv, (1, 0, 2)), w_out,
+        keep(tokens), keep(dest.reshape(1, ROWS)), keep(segment_ids.reshape(1, ROWS)),
+        keep(gain.reshape(1, WIDTH)),
+        keep(jnp.transpose(w_qkv, (1, 0, 2))), keep(w_out),
     )
 
 

time: 50.9 us -> 48 us (0.943)
  Pallas kernels: 48.9 us -> 47.1 us
  local copies, waits for them, and re-layouts: 1.87 us -> 0.8 us
    pallas_call x1, Pallas kernels: 48.9 us -> 47.1 us  [shards(): pl.pallas_call(layer, out_shape=jax.ShapeDtypeStruct((ROWS, 1024), BF16),...]
    unnamed x1, local copies, waits for them, and re-layouts: 1.87 us -> 0.8 us
where the time goes in v1:
time: 48 us; the launch traced here: 47.9 us
  Pallas kernels  47.1 us (98%)
  local copies, waits for them, and re-layouts  0.8 us (2%)
    pallas_call x1, Pallas kernels, shards(): pl.pallas_call(layer, out_shape=jax.ShapeDtypeStruct((ROWS, 1024), BF16),...  47.1 us

profile of v1, /device:TPU:1, one launch (start us, length us, event | category | flops | bytes accessed | tf_op | source)
XLA Modules:
  0.0 47.9 jit_solution(3276016421234221194)
XLA Ops:
  0.0 47.1 %shard_map.64 = bf16[256,1024]{1,0:T(8,128)(2,1)S(1)} custom-call(bf16[256,2048]{1,0:T(8,128)(2,1)} %tok_hbm.1, s32[1,256]{1,0:T(1,128)} %bitcast.6, s32[1,256]{1,0:T(1,128)} %bitcast.7, f32[1,2048]{1,0:T(1,128)} %bitcast.5, bf16[3,2048,512]{2,1,0:T(8,128)(2,1)} %bitcast.4, bf16[512,2048]{1,0:T(8,128)(2,1)} %wout_hbm.1), custom_call_target="tpu_custom_call" | custom-call | tf_op jit(solution)/shard_map/pallas_call | solution.py:399
  47.1 0.8 %copy.8 = bf16[256,1024]{1,0:T(8,128)(2,1)} copy(bf16[256,1024]{1,0:T(8,128)(2,1)S(1)} %shard_map.64) | data formatting | bytes 1048576

commit v2 on v1

--- a/solution.py
+++ b/solution.py
@@ -23,7 +23,7 @@
 SCORE = DH ** (-0.5) * math.log2(math.e)
 WAVES = ((0,), (1, 7), (2, 6), (3, 5, 4))
 ORDER = tuple(oz for wave in WAVES for oz in wave)
-EARLY = 4
+PARTS = (0, 3, 5, 8)
 
 
 def iota(shape, dim):
@@ -195,48 +195,53 @@
                 stage[pl.ds(group * NXY * CHUNKS + j, NXY, stride=CHUNKS), :].astype(BF16)
             )
 
-    def collect(first):
-        base = (first // EARLY) * 128
-        for group in range(first, first + EARLY):
+    def collect(part):
+        first, last = PARTS[part], PARTS[part + 1]
+        line = 2 * NXY * first
+        for group in range(first, last):
             block = pl.ds(group * NXY, NXY)
             drain(recv.at[block], row_recv.at[group])
             remote(
                 recv.at[block], recv_sib.at[block], sib_send, sib_recv.at[group], me, other
             ).start()
-            unpack(group, recv, base + (group - first) * NXY)
-        for group in range(first, first + EARLY):
+            unpack(group, recv, line)
+            line += NXY
+        for group in range(first, last):
             drain(recv_sib.at[pl.ds(group * NXY, NXY)], sib_recv.at[group])
-            unpack(group, recv_sib, base + 64 + (group - first) * NXY)
-
-    def project(part, own, half):
-        lines = slice(half * 128, (half + 1) * 128)
+            unpack(group, recv_sib, line)
+            line += NXY
+
+    def span(number):
+        return pl.ds(2 * NXY * PARTS[number], 2 * NXY * (PARTS[number + 1] - PARTS[number]))
+
+    def project(part, own, number):
+        lines = span(number)
         own[lines, :] = mm(xs[lines, :], wqkv[part]).astype(BF16)
 
-    def send_halo(own, halo, half, send_sem, recv_sem):
-        lines = pl.ds(half * 128, 128)
+    def send_halo(own, halo, number, send_sem, recv_sem):
+        lines = span(number)
         for side, peer in ((1, left), (0, right)):
             remote(
-                own.at[lines], halo.at[side, lines], send_sem, recv_sem.at[side, half], peer, core
+                own.at[lines], halo.at[side, lines], send_sem, recv_sem.at[side, number], peer, core
             ).start()
 
-    collect(0)
-    load_w[1].wait()
-    load_w[2].wait()
-    project(1, k_own, 0)
-    send_halo(k_own, k_halo, 0, k_send, k_recv)
-    project(2, v_own, 0)
-    send_halo(v_own, v_halo, 0, v_send, v_recv)
-
-    collect(EARLY)
-    project(1, k_own, 1)
-    send_halo(k_own, k_halo, 1, k_send, k_recv)
-    project(2, v_own, 1)
+    last = len(PARTS) - 2
+    for number in range(last + 1):
+        collect(number)
+        if number == 0:
+            load_w[1].wait()
+            load_w[2].wait()
+        project(1, k_own, number)
+        send_halo(k_own, k_halo, number, k_send, k_recv)
+        project(2, v_own, number)
+        if number < last:
+            send_halo(v_own, v_halo, number, v_send, v_recv)
 
     drain(posb.at[pl.ds(0, 240)], pos_sem.at[3])
     pieces = []
-    for first in (0, EARLY):
+    for number in range(last + 1):
         for who in (core, other):
-            for oz in ORDER[first:first + EARLY]:
+            for oz in ORDER[PARTS[number]:PARTS[number + 1]]:
                 pieces.append(posb[pl.ds(who * NZ + (z + NZ - oz) % NZ, NXY, stride=16), :])
     table = jnp.concatenate(pieces, axis=0).astype(BF16)
     my_lane = jnp.where(iota((8, 128), 1) == me, 1.0, 0.0).astype(BF16)
@@ -291,7 +296,7 @@
                 crs_sem.at[0], crs_sem.at[1], partner * size + i, core,
             ).start()
         start += lines
-    send_halo(v_own, v_halo, 1, v_send, v_recv)
+    send_halo(v_own, v_halo, last, v_send, v_recv)
     remote(
         wout_hbm.at[:, pl.ds(pl.multiple_of(other * 1024, 1024), 1024)], wo_sib,
         wo_sem.at[0], wo_sem.at[1], me, other,
@@ -325,9 +330,9 @@
         same = own_col == ids_halo[side][0:1, :]
         bias[:, (side + 1) * ROWS:(side + 2) * ROWS] = jnp.where(same & edge[side], 0.0, -jnp.inf)
 
-    for half in range(2):
+    for number in range(last + 1):
         for side in range(2):
-            drain(k_halo.at[side, pl.ds(half * 128, 128)], k_recv.at[side, half])
+            drain(k_halo.at[side, span(number)], k_recv.at[side, number])
     drain(crs, crs_sem.at[1])
     far[...] = mm(line_up[...], crs[...]).astype(BF16)
     lift = (iota((8, 64), 1) // 16 + 4).astype(F32)[0:1, :]
@@ -353,9 +358,9 @@
         tot[h] = total
 
     load_wo.wait()
-    for half in range(2):
+    for number in range(last + 1):
         for side in range(2):
-            drain(v_halo.at[side, pl.ds(half * 128, 128)], v_recv.at[side, half])
+            drain(v_halo.at[side, span(number)], v_recv.at[side, number])
     for half in range(2):
         for h in (half * 2, half * 2 + 1):
             total = acc[h]
@@ -416,7 +421,7 @@
             V((HEADS, ROWS, 128), F32), V((HEADS, ROWS, 128), F32), V((HEADS, ROWS, 128), F32),
             V((HEADS, 2, ROWS, ROWS), BF16), V((2, ROWS, 256), BF16), V((2, ROWS, 256), BF16),
             dma((8,)), dma, dma((NZ,)), dma, dma((NZ,)), pltpu.SemaphoreType.REGULAR((NZ,)),
-            dma((4,)), dma((2,)), dma, dma((2, 2)), dma, dma((2, 2)), dma((2,)), dma((2,)), dma((3,)),
+            dma((4,)), dma((2,)), dma, dma((2, 6)), dma, dma((2, 6)), dma((2,)), dma((2,)), dma((3,)),
         ],
         compiler_params=pltpu.CompilerParams(collective_id=0, has_side_effects=True, vmem_limit_bytes=40 * 2**20),
     )(

time: 48 us -> 45.1 us (0.940)
  Pallas kernels: 47.1 us -> 44.2 us
    pallas_call x1, Pallas kernels: 47.1 us -> 44.2 us  [shards(): pl.pallas_call(layer, out_shape=jax.ShapeDtypeStruct((ROWS, 1024), BF16),...]
where the time goes in v2:
time: 45.1 us; the launch traced here: 45 us
  Pallas kernels  44.2 us (98%)
  local copies, waits for them, and re-layouts  0.8 us (2%)
    pallas_call x1, Pallas kernels, shards(): pl.pallas_call(layer, out_shape=jax.ShapeDtypeStruct((ROWS, 1024), BF16),...  44.2 us

profile of v2, /device:TPU:1, one launch (start us, length us, event | category | flops | bytes accessed | tf_op | source)
XLA Modules:
  0.0 45.0 jit_solution(6669616160061714420)
XLA Ops:
  0.0 44.2 %shard_map.64 = bf16[256,1024]{1,0:T(8,128)(2,1)S(1)} custom-call(bf16[256,2048]{1,0:T(8,128)(2,1)} %tok_hbm.1, s32[1,256]{1,0:T(1,128)} %bitcast.6, s32[1,256]{1,0:T(1,128)} %bitcast.7, f32[1,2048]{1,0:T(1,128)} %bitcast.5, bf16[3,2048,512]{2,1,0:T(8,128)(2,1)} %bitcast.4, bf16[512,2048]{1,0:T(8,128)(2,1)} %wout_hbm.1), custom_call_target="tpu_custom_call" | custom-call | tf_op jit(solution)/shard_map/pallas_call | solution.py:404
  44.2 0.8 %copy.8 = bf16[256,1024]{1,0:T(8,128)(2,1)} copy(bf16[256,1024]{1,0:T(8,128)(2,1)S(1)} %shard_map.64) | data formatting | bytes 1048576

commit v3 on v2

--- a/solution.py
+++ b/solution.py
@@ -43,7 +43,7 @@
     dest_ref, seg_ref, gain_ref, tok, wqkv, wo_own, wo_sib, stage, send, recv, recv_sib, xs,
     posa_src, posa, posb_src, posb, place, pool,
     k_own, v_own, q_raw, q_own, ids_src, ids_halo, k_halo, v_halo,
-    crs_src, crs, line_up, far, bias, top, tot, acc, prob, at_own, at_sib,
+    crs_src, crs, line_up, far, bias, top, tot, acc, prob, at_own, at_sib, sums, far_sum,
     load_sem, row_send, row_recv, sib_send, sib_recv, go,
     pos_sem, ids_sem, k_send, k_recv, v_send, v_recv, crs_sem, wo_sem, at_sem,
 ):
@@ -333,55 +333,81 @@
     for number in range(last + 1):
         for side in range(2):
             drain(k_halo.at[side, span(number)], k_recv.at[side, number])
-    drain(crs, crs_sem.at[1])
-    far[...] = mm(line_up[...], crs[...]).astype(BF16)
-    lift = (iota((8, 64), 1) // 16 + 4).astype(F32)[0:1, :]
 
     for h in range(HEADS):
         scores = [
             fine(h, head(k_halo.at[side], h), bias[:, (side + 1) * ROWS:(side + 2) * ROWS])
             for side in range(2)
         ]
-        scores.append(fine(h, far[h * 64:(h + 1) * 64, 0:128], lift))
         old = top[h][:, 0:1]
         best = old
         for score in scores:
             best = jnp.maximum(best, jnp.max(score, axis=-1, keepdims=True))
         fade = jnp.exp2(old - best)
-        weight = jnp.exp2(scores[2] - best)
-        total = tot[h] * fade + jnp.sum(weight, axis=-1, keepdims=True)
-        acc[h] = acc[h] * fade + mm(weight.astype(BF16), far[h * 64:(h + 1) * 64, 128:256])
+        total = tot[h] * fade
+        acc[h] = acc[h] * fade
         for side in range(2):
             weight = jnp.exp2(scores[side] - best)
             total = total + jnp.sum(weight, axis=-1, keepdims=True)
             prob[h, side] = weight.astype(BF16)
         tot[h] = total
-
-    load_wo.wait()
-    for number in range(last + 1):
+        top[h] = jnp.broadcast_to(best, (ROWS, 128))
+
+    drain(crs, crs_sem.at[1])
+    far[...] = mm(line_up[...], crs[...]).astype(BF16)
+    lift = (iota((8, 64), 1) // 16 + 4).astype(F32)[0:1, :]
+    for h in range(HEADS):
+        score = fine(h, far[h * 64:(h + 1) * 64, 0:128], lift)
+        old = top[h][:, 0:1]
+        best = jnp.maximum(old, jnp.max(score, axis=-1, keepdims=True))
+        fade = jnp.exp2(old - best)
+        weight = jnp.exp2(score - best)
+        tot[h] = tot[h] * fade + jnp.sum(weight, axis=-1, keepdims=True)
+        top[h] = jnp.broadcast_to(fade, (ROWS, 128))
+        far_sum[h] = mm(weight.astype(BF16), far[h * 64:(h + 1) * 64, 128:256])
+
+    for number in range(last):
         for side in range(2):
             drain(v_halo.at[side, span(number)], v_recv.at[side, number])
+    for h in range(HEADS):
+        total = acc[h]
+        for side in range(2):
+            total = total + mm(prob[h, side, :, 0:128], v_halo[side, 0:128, h * 128:(h + 1) * 128])
+        acc[h] = total
+    load_wo.wait()
+    for side in range(2):
+        drain(v_halo.at[side, span(last)], v_recv.at[side, last])
     for half in range(2):
         for h in (half * 2, half * 2 + 1):
             total = acc[h]
             for side in range(2):
-                total = total + mm(prob[h, side], head(v_halo.at[side], h))
+                total = total + mm(prob[h, side, :, 128:256], v_halo[side, 128:256, h * 128:(h + 1) * 128])
+            total = total * top[h] + far_sum[h]
             at_own[half, :, (h % 2) * 128:(h % 2 + 1) * 128] = (total / tot[h]).astype(BF16)
         remote(
             at_own.at[half], at_sib.at[half], at_sem.at[0], at_sem.at[1 + half], me, other
         ).start()
 
+    for half in range(2):
+        lines = slice(half * 256, (half + 1) * 256)
+        for part in range(4):
+            cols = slice(part * 256, (part + 1) * 256)
+            product = mm(at_own[half], wo_own[lines, cols])
+            if half == 0:
+                sums[:, cols] = product
+            else:
+                sums[:, cols] = sums[:, cols] + product
     drain(wo_sib, wo_sem.at[1])
     for half in range(2):
+        lines = slice(half * 256, (half + 1) * 256)
         drain(at_sib.at[half], at_sem.at[1 + half])
-    for part in range(4):
-        cols = slice(part * 256, (part + 1) * 256)
-        total = jnp.zeros((ROWS, 256), F32)
-        for half in range(2):
-            lines = slice(half * 256, (half + 1) * 256)
-            total = total + mm(at_own[half], wo_own[lines, cols])
-            total = total + mm(at_sib[half], wo_sib[lines, cols])
-        out_ref[:, cols] = total.astype(BF16)
+        for part in range(4):
+            cols = slice(part * 256, (part + 1) * 256)
+            total = sums[:, cols] + mm(at_sib[half], wo_sib[lines, cols])
+            if half == 0:
+                sums[:, cols] = total
+            else:
+                out_ref[:, cols] = total.astype(BF16)
 
     drain(send.at[pl.ds(0, SHARDS - 1)], row_send)
     drain(posa.at[pl.ds(0, NZ - 1)], pos_sem.at[0])
@@ -420,6 +446,7 @@
             V((ROWS, 3 * ROWS), F32),
             V((HEADS, ROWS, 128), F32), V((HEADS, ROWS, 128), F32), V((HEADS, ROWS, 128), F32),
             V((HEADS, 2, ROWS, ROWS), BF16), V((2, ROWS, 256), BF16), V((2, ROWS, 256), BF16),
+            V((ROWS, 1024), F32), V((HEADS, ROWS, 128), F32),
             dma((8,)), dma, dma((NZ,)), dma, dma((NZ,)), pltpu.SemaphoreType.REGULAR((NZ,)),
             dma((4,)), dma((2,)), dma, dma((2, 6)), dma, dma((2, 6)), dma((2,)), dma((2,)), dma((3,)),
         ],

time: 45.1 us -> 44.1 us (0.978)
  Pallas kernels: 44.2 us -> 43.2 us
    pallas_call x1, Pallas kernels: 44.2 us -> 43.2 us  [shards(): pl.pallas_call(layer, out_shape=jax.ShapeDtypeStruct((ROWS, 1024), BF16),...]
where the time goes in v3:
time: 44.1 us; the launch traced here: 44 us
  Pallas kernels  43.2 us (98%)
  local copies, waits for them, and re-layouts  0.8 us (2%)
    pallas_call x1, Pallas kernels, shards(): pl.pallas_call(layer, out_shape=jax.ShapeDtypeStruct((ROWS, 1024), BF16),...  43.2 us

profile of v3, /device:TPU:1, one launch (start us, length us, event | category | flops | bytes accessed | tf_op | source)
XLA Modules:
  0.0 44.0 jit_solution(16133243399243098413)
XLA Ops:
  0.0 43.2 %shard_map.64 = bf16[256,1024]{1,0:T(8,128)(2,1)S(1)} custom-call(bf16[256,2048]{1,0:T(8,128)(2,1)} %tok_hbm.1, s32[1,256]{1,0:T(1,128)} %bitcast.6, s32[1,256]{1,0:T(1,128)} %bitcast.7, f32[1,2048]{1,0:T(1,128)} %bitcast.5, bf16[3,2048,512]{2,1,0:T(8,128)(2,1)} %bitcast.4, bf16[512,2048]{1,0:T(8,128)(2,1)} %wout_hbm.1), custom_call_target="tpu_custom_call" | custom-call | tf_op jit(solution)/shard_map/pallas_call | solution.py:430
  43.2 0.8 %copy.8 = bf16[256,1024]{1,0:T(8,128)(2,1)} copy(bf16[256,1024]{1,0:T(8,128)(2,1)S(1)} %shard_map.64) | data formatting | bytes 1048576

commit v4 on v3

--- a/solution.py
+++ b/solution.py
@@ -384,9 +384,11 @@
                 total = total + mm(prob[h, side, :, 128:256], v_halo[side, 128:256, h * 128:(h + 1) * 128])
             total = total * top[h] + far_sum[h]
             at_own[half, :, (h % 2) * 128:(h % 2 + 1) * 128] = (total / tot[h]).astype(BF16)
-        remote(
-            at_own.at[half], at_sib.at[half], at_sem.at[0], at_sem.at[1 + half], me, other
-        ).start()
+            block = pl.ds((h % 2) * 128, 128)
+            remote(
+                at_own.at[half, :, block], at_sib.at[half, :, block], at_sem.at[0],
+                at_sem.at[1 + half], me, other,
+            ).start()
 
     for half in range(2):
         lines = slice(half * 256, (half + 1) * 256)

time: 44.1 us -> 44.3 us (level)
  no operation moved by 1% of the time
where the time goes in v4:
time: 44.3 us; the launch traced here: 44.2 us
  Pallas kernels  43.4 us (98%)
  local copies, waits for them, and re-layouts  0.8 us (2%)
    pallas_call x1, Pallas kernels, shards(): pl.pallas_call(layer, out_shape=jax.ShapeDtypeStruct((ROWS, 1024), BF16),...  43.4 us

profile of v4, /device:TPU:1, one launch (start us, length us, event | category | flops | bytes accessed | tf_op | source)
XLA Modules:
  0.0 44.2 jit_solution(15926009580793380868)
XLA Ops:
  0.0 43.4 %shard_map.64 = bf16[256,1024]{1,0:T(8,128)(2,1)S(1)} custom-call(bf16[256,2048]{1,0:T(8,128)(2,1)} %tok_hbm.1, s32[1,256]{1,0:T(1,128)} %bitcast.6, s32[1,256]{1,0:T(1,128)} %bitcast.7, f32[1,2048]{1,0:T(1,128)} %bitcast.5, bf16[3,2048,512]{2,1,0:T(8,128)(2,1)} %bitcast.4, bf16[512,2048]{1,0:T(8,128)(2,1)} %wout_hbm.1), custom_call_target="tpu_custom_call" | custom-call | tf_op jit(solution)/shard_map/pallas_call | solution.py:432
  43.4 0.8 %copy.8 = bf16[256,1024]{1,0:T(8,128)(2,1)} copy(bf16[256,1024]{1,0:T(8,128)(2,1)S(1)} %shard_map.64) | data formatting | bytes 1048576
